TPU v7x, 256 devices: a whole 4x4x8 slice. The times are simulated.
256 devices in a mesh: dp: 32 (over x, z_hi, core), expert: 8 (over y, z_lo).
Axes of the slice: x: 4, y: 4, z: 8 (z_hi: 4, z_lo: 2; z = z_hi * 2 + z_lo), core: 2. Of those that a mesh axis runs over, the one named last changes fastest.
Arguments:
- tokens: bfloat16 [32768, 4096], P(('dp', 'expert')), may hold values from -6 to 6
- cotangent: bfloat16 [32768, 4096], P(('dp', 'expert')), may hold values from -1.1953125 to 1.1953125
- expert_ids: int32 [32768, 2], P(('dp', 'expert')), may hold values from 0 to 63, as said below
- gate_probs: bfloat16 [32768, 2], P(('dp', 'expert')), may hold values from 0.049804688 to 1
- gate_w: bfloat16 [8, 7168, 4096], P('expert', 'dp'), may hold values from -0.09375 to 0.09375
- up_w: bfloat16 [8, 7168, 4096], P('expert', 'dp'), may hold values from -0.09375 to 0.09375
- down_w: bfloat16 [8, 7168, 4096], P('expert', 'dp'), may hold values from -0.0625 to 0.0625
Outputs:
- grad_gate: bfloat16 [8, 7168, 4096], P('expert', 'dp')
- grad_up: bfloat16 [8, 7168, 4096], P('expert', 'dp')
- grad_down: bfloat16 [8, 7168, 4096], P('expert', 'dp')
- grad_probs: float32 [32768, 2], P(('dp', 'expert'))
Inputs may be any that keep to these rules, and one draw needn't show every extreme that they name: `expert_ids`: each token names two different experts. Split the rows into aligned blocks of 128 (the rows of one device) and those into aligned runs of 8 blocks: a block names any one expert below 8 at most 4 times, and a run names it at most 16 times; in every draw some block reaches 4 and some run reaches 16.
All inputs are finite; a program needn't handle non-finite values.
Results may differ from a plain program's by a relative error of at most 0.015.
Values may be sent and summed in bfloat16 or wider, within the bound.
No kernel may reach another device: no remote copies, remote signals or barrier semaphores. Data moves between devices by JAX's collectives and lax.ppermute only.
A program may use at most 128 MiB of HBM per device.

v0:
```python
import jax
import jax.numpy as jnp
from jax import lax
from jax.sharding import PartitionSpec as P

ROW_CAPACITY = 4


def contract_rows(left, right):
    return lax.dot_general(
        left, right, (((0,), (0,)), ((), ())), preferred_element_type=jnp.float32
    )


def contract_cols(left, right):
    return lax.dot_general(
        left, right, (((1,), (1,)), ((), ())), preferred_element_type=jnp.float32
    )


def shards(tokens, cotangent, expert_ids, gate_probs, gate_w, up_w, down_w):
    owners = lax.axis_size("expert")
    slots = owners * ROW_CAPACITY
    flat_ids = expert_ids.reshape(-1)
    marks = (flat_ids[:, None] == jnp.arange(owners, dtype=jnp.int32)[None, :]).astype(jnp.int32)
    before = jnp.cumsum(marks, axis=0) - marks
    ranking = jnp.sum(before * marks, axis=1)
    target = jnp.where(jnp.sum(marks, axis=1) > 0, flat_ids * ROW_CAPACITY + ranking, -1)
    routing = (target[None, :] == jnp.arange(slots, dtype=jnp.int32)[:, None]).astype(jnp.float32)
    per_token = routing.reshape(slots, -1, 2).sum(axis=2).astype(jnp.bfloat16)
    send_x = jnp.dot(per_token, tokens, preferred_element_type=jnp.float32).astype(jnp.bfloat16)
    send_dy = jnp.dot(per_token, cotangent, preferred_element_type=jnp.float32).astype(jnp.bfloat16)
    send_p = jnp.dot(
        routing.astype(jnp.bfloat16), gate_probs.reshape(-1), preferred_element_type=jnp.float32
    ).astype(jnp.bfloat16)
    got_x, got_dy, got_p = (
        lax.all_to_all(
            send_x.reshape(owners, ROW_CAPACITY, -1),
            "expert",
            split_axis=0,
            concat_axis=0,
            tiled=True,
        ),
        lax.all_to_all(
            send_dy.reshape(owners, ROW_CAPACITY, -1),
            "expert",
            split_axis=0,
            concat_axis=0,
            tiled=True,
        ),
        lax.all_to_all(
            send_p.reshape(owners, ROW_CAPACITY), "expert", split_axis=0, concat_axis=0, tiled=True
        ),
    )
    rows_x = got_x.reshape(slots, -1)
    rows_dy = got_dy.reshape(slots, -1)
    rows_p = got_p.reshape(slots)
    gate_local = gate_w[0]
    up_local = up_w[0]
    down_local = down_w[0]
    piece_x = lax.all_gather(rows_x, "dp", axis=0, tiled=True)
    piece_dy = lax.all_gather(rows_dy, "dp", axis=0, tiled=True)
    piece_p = lax.all_gather(rows_p, "dp", axis=0, tiled=True)
    weight_p = piece_p.astype(jnp.float32)[:, None]
    gate_pre = contract_cols(piece_x, gate_local)
    up_pre = contract_cols(piece_x, up_local)
    sigma = jax.nn.sigmoid(gate_pre)
    hidden = (gate_pre * sigma * up_pre).astype(jnp.bfloat16)
    pulled = contract_cols(piece_dy, down_local)
    router = jnp.sum(hidden.astype(jnp.float32) * pulled, axis=1)
    scaled_dy = (weight_p * piece_dy.astype(jnp.float32)).astype(jnp.bfloat16)
    d_hidden = weight_p * pulled
    d_gate = (d_hidden * up_pre * sigma * (1.0 + gate_pre * (1.0 - sigma))).astype(jnp.bfloat16)
    d_up = (d_hidden * gate_pre * sigma).astype(jnp.bfloat16)
    new_gate = contract_rows(d_gate, piece_x)
    new_up = contract_rows(d_up, piece_x)
    new_down = contract_rows(hidden, scaled_dy)
    router_rows = lax.psum_scatter(router, "dp", scatter_dimension=0, tiled=True)
    returned = lax.all_to_all(
        router_rows.reshape(owners, ROW_CAPACITY), "expert", split_axis=0, concat_axis=0, tiled=True
    )
    grad_flat = jnp.dot(returned.reshape(slots), routing, precision=lax.Precision.HIGHEST)
    grad_gate = new_gate.astype(jnp.bfloat16)[None]
    grad_up = new_up.astype(jnp.bfloat16)[None]
    grad_down = new_down.astype(jnp.bfloat16)[None]
    return (grad_gate, grad_up, grad_down, grad_flat.reshape(-1, 2))


def solution(mesh):
    in_specs = (
        P(("dp", "expert"), None),
        P(("dp", "expert"), None),
        P(("dp", "expert"), None),
        P(("dp", "expert"), None),
        P("expert", "dp", None),
        P("expert", "dp", None),
        P("expert", "dp", None),
    )
    out_specs = (
        P("expert", "dp", None),
        P("expert", "dp", None),
        P("expert", "dp", None),
        P(("dp", "expert"), None),
    )
    return jax.shard_map(shards, mesh=mesh, in_specs=in_specs, out_specs=out_specs, check_vma=False)
```

profile of v0, /device:TPU:8, one launch (start us, length us, event | category | flops | bytes accessed | tf_op | source)
XLA Modules:
  0.0 299.6 jit_solution(5309269911778163074)
XLA Ops:
  7.2 0.0 copy-start
  7.2 0.0 all-gather.5.cloned.1.call-start
  7.2 0.9 copy.36
  8.1 0.1 eq.64
  8.3 0.1 eq.68
  8.4 0.6 reduce-window.6
  9.0 0.2 slice_reduce_fusion
  9.3 0.1 fusion.23
  9.4 0.1 reduce_sum.40
  9.5 0.2 gt.17
  9.7 0.1 copy.41
  9.8 0.1 copy.40
  9.8 0.7 add_select_fusion
  10.6 1.5 convolution_convert_fusion.2
  12.1 0.1 reshape.108
  12.2 11.8 %all_to_all.29 = bf16[8,4,4096]{2,1,0:T(4,128)(2,1)S(1)} all-to-all(bf16[8,4,4096]{2,1,0:T(4,128)(2,1)S(1)} %reshape.108), channel_id=1, replica_groups=mesh['dp'=32,'expert'=8] {'expert'}, dimensions={0} | all-to-all | bytes 524288 | tf_op jit(solution)/shard_map/all_to_all | solution.py:37
  24.0 0.8 reshape.109
  24.8 0.0 all-gather.5.cloned.1.call-update
  24.8 0.0 all-gather.3.cloned.1.call-start
  24.8 1.5 convolution_convert_fusion.3
  26.3 0.1 reshape.106
  26.5 9.6 %all_to_all.30 = bf16[8,4,4096]{2,1,0:T(4,128)(2,1)S(1)} all-to-all(bf16[8,4,4096]{2,1,0:T(4,128)(2,1)S(1)} %reshape.106), channel_id=1, replica_groups=mesh['dp'=32,'expert'=8] {'expert'}, dimensions={0} | all-to-all | bytes 524288 | tf_op jit(solution)/shard_map/all_to_all | solution.py:44
  36.0 0.8 reshape.107
  36.8 0.0 all-gather.3.cloned.1.call-update
  36.8 0.8 copy.38
  37.6 0.1 reshape.116
  37.8 0.1 fusion.12
  37.9 0.7 all_to_all.24
  38.6 5.0 %all-to-all-start = ((bf16[8,1,4]{2,1,0:T(2,128)(2,1)}), bf16[8,1,4]{2,1,0:T(2,128)(2,1)S(1)}, u32[]{:S(2)}, u32[]{:S(2)}) async-start(bf16[8,1,4]{2,1,0:T(2,128)(2,1)} %all_to_all.24), calls=%async_computation | async-start | bytes 8192 | tf_op jit(solution)/shard_map/all_to_all | solution.py:51
  43.6 1.3 fusion.29
  46.1 2.1 all-to-all-done
  48.3 0.1 reshape.111
  48.4 0.2 dynamic-update-slice
  48.6 77.6 %all-reduce = bf16[1024]{0:T(1024)(128)(2,1)S(1)} all-reduce(bf16[1024]{0:T(1024)(128)(2,1)S(1)} %dynamic-update-slice), channel_id=1, replica_groups=mesh['dp'=32,'expert'=8] {'dp'}, use_global_device_ids=true, to_apply=%add | all-reduce | flops 1024 | bytes 4096
  126.2 0.0 all-gather.5.cloned.1.call-done
  126.2 0.0 copy-start.1
  126.2 0.0 copy-start.3
  126.2 6.8 %fusion.6 = f32[1024,224]{0,1:T(8,128)S(1)} fusion(bf16[1024,4096]{1,0:T(8,128)(2,1)} %all-gather.5.cloned.1.call-done, bf16[1,224,4096]{2,1,0:T(8,128)(2,1)} %param.11), kind=kOutput, calls=%fused_computation.11 | convolution fusion | flops 1879048192 | bytes 11141120 | tf_op jit(solution)/shard_map/dot_general | solution.py:16
  133.0 0.0 copy-done.1
  133.0 0.1 copy-done.3
  133.1 3.6 %fusion.8 = f32[1024,224]{0,1:T(8,128)} fusion(bf16[1024,4096]{1,0:T(8,128)(2,1)S(1)} %copy-done.1, bf16[1,224,4096]{2,1,0:T(8,128)(2,1)S(1)} %copy-done.3), kind=kOutput, calls=%fused_computation.13 | convolution fusion | flops 1879048192 | bytes 11141120 | tf_op jit(solution)/shard_map/dot_general | solution.py:16
  136.7 48.4 %all-gather.3.cloned.1.call-done = bf16[1024,4096]{1,0:T(8,128)(2,1)} async-done(((bf16[32,4096]{1,0:T(8,128)(2,1)}), bf16[1024,4096]{1,0:T(8,128)(2,1)}) %all-gather.3.cloned.1.call-update) | async-done | bytes 8388624 | tf_op jit(solution)/shard_map/all_gather | solution.py:62
  185.1 0.0 copy-done
  185.1 7.2 %multiply_reduce_fusion = (f32[1024]{0:T(1024)S(1)}, bf16[1024,224]{0,1:T(8,128)(2,1)S(1)}, f32[1024,224]{0,1:T(8,128)}) fusion(f32[1024,224]{0,1:T(8,128)} %fusion.8, f32[1024,224]{0,1:T(8,128)S(1)} %fusion.6, bf16[1024,4096]{1,0:T(8,128)(2,1)} %all-gather.3.cloned.1.call-done, bf16[1,224,4096]{2,1,0:T(8,128)(2,1)S(1)} %copy-done), kind=kOutput, calls=%fused_computation.19 | convolution fusion | flops 1881111552 | bytes 13438976 | tf_op jit(solution)/shard_map/dot_general | solution.py:16
  192.3 75.1 %all-reduce.1 = f32[1024]{0:T(1024)S(1)} all-reduce(f32[1024]{0:T(1024)S(1)} %get-tuple-element.6), channel_id=2, replica_groups=mesh['dp'=32,'expert'=8] {'dp'}, use_global_device_ids=true, to_apply=%region_6.7.clone | all-reduce | flops 1024 | bytes 8192
  267.4 0.1 dynamic-slice.2
  267.4 0.7 all_to_all.22
  268.1 4.8 %all-to-all-start.3 = ((f32[8,1,4]{2,1,0:T(1,128)}), f32[8,1,4]{2,1,0:T(1,128)S(1)}, u32[]{:S(2)}, u32[]{:S(2)}) async-start(f32[8,1,4]{2,1,0:T(1,128)} %bitcast.10), calls=%async_computation.3 | async-start | bytes 8192 | tf_op jit(solution)/shard_map/all_to_all | solution.py:79
  272.9 0.0 copy-start.4
  272.9 7.5 %fusion.3 = bf16[1,224,4096]{2,1,0:T(8,128)(2,1)} fusion(bf16[1024,4096]{1,0:T(8,128)(2,1)} %all-gather.5.cloned.1.call-done, f32[1024,224]{0,1:T(8,128)S(1)} %fusion.6, f32[1024,224]{0,1:T(8,128)} %fusion.8, f32[1024,224]{0,1:T(8,128)} %get-tuple-element.12, f32[1024]{0:T(1024)S(1)} %convert_element_type.63), kind=kOutput, calls=%fused_computation.6 | convolution fusion | flops 1882488832 | bytes 12980224 | tf_op jit(solution)/shard_map/dot_general | solution.py:10
  280.4 0.0 copy-done.4
  280.4 0.0 copy-start.2
  280.4 6.9 %fusion.4 = bf16[1,224,4096]{2,1,0:T(8,128)(2,1)} fusion(bf16[1024,4096]{1,0:T(8,128)(2,1)} %all-gather.5.cloned.1.call-done, f32[1024,224]{0,1:T(8,128)S(1)} %fusion.6, f32[1024,224]{0,1:T(8,128)S(1)} %copy-done.4, f32[1024]{0:T(1024)S(1)} %convert_element_type.63), kind=kOutput, calls=%fused_computation.7 | convolution fusion | flops 1881571328 | bytes 12062720 | tf_op jit(solution)/shard_map/dot_general | solution.py:10
  287.3 0.0 copy-done.2
  287.3 3.5 %fusion.5 = bf16[1,224,4096]{2,1,0:T(8,128)(2,1)} fusion(bf16[1024,224]{0,1:T(8,128)(2,1)S(1)} %get-tuple-element.7, bf16[1024,4096]{1,0:T(8,128)(2,1)S(1)} %copy-done.2, f32[1024]{0:T(1024)S(1)} %convert_element_type.63), kind=kOutput, calls=%fused_computation.8 | convolution fusion | flops 1892548608 | bytes 10686464 | tf_op jit(solution)/shard_map/dot_general | solution.py:10
  290.8 0.0 all-to-all-done.3
  290.9 0.5 broadcast.75
  291.4 0.7 reduce.6
  292.0 0.1 reshape.118
  292.1 0.7 fusion.18
  (8 shorter events, 0.1 us)
Async XLA Ops:
  7.2 177.9 %copy-start = (bf16[1,224,4096]{2,1,0:T(8,128)(2,1)S(1)}, bf16[1,224,4096]{2,1,0:T(8,128)(2,1)}, u32[]{:S(2)}) copy-start(bf16[1,224,4096]{2,1,0:T(8,128)(2,1)} %param.13) | copy-start | bytes 5505028
  7.2 119.0 %all-gather.5.cloned.1.call-start = ((), (), s32[]{:S(2)}) async-start(), calls=%async_computation.5 | async-start | bytes 8650752 | tf_op jit(solution)/shard_map/all_gather | solution.py:61
  24.8 160.3 %all-gather.3.cloned.1.call-start = ((), (), s32[]{:S(2)}) async-start(), calls=%async_computation.4 | async-start | bytes 8650752 | tf_op jit(solution)/shard_map/all_gather | solution.py:62
  38.6 9.7 %all-to-all-start = ((bf16[8,1,4]{2,1,0:T(2,128)(2,1)}), bf16[8,1,4]{2,1,0:T(2,128)(2,1)S(1)}, u32[]{:S(2)}, u32[]{:S(2)}) async-start(bf16[8,1,4]{2,1,0:T(2,128)(2,1)} %all_to_all.24), calls=%async_computation | async-start | bytes 8192 | tf_op jit(solution)/shard_map/all_to_all | solution.py:51
  126.2 6.8 %copy-start.1 = (bf16[1024,4096]{1,0:T(8,128)(2,1)S(1)}, bf16[1024,4096]{1,0:T(8,128)(2,1)}, u32[]{:S(2)}) copy-start(bf16[1024,4096]{1,0:T(8,128)(2,1)} %all-gather.5.cloned.1.call-done) | copy-start | bytes 25165828
  126.2 6.9 %copy-start.3 = (bf16[1,224,4096]{2,1,0:T(8,128)(2,1)S(1)}, bf16[1,224,4096]{2,1,0:T(8,128)(2,1)}, u32[]{:S(2)}) copy-start(bf16[1,224,4096]{2,1,0:T(8,128)(2,1)} %param.12) | copy-start | bytes 5505028
  268.1 22.7 %all-to-all-start.3 = ((f32[8,1,4]{2,1,0:T(1,128)}), f32[8,1,4]{2,1,0:T(1,128)S(1)}, u32[]{:S(2)}, u32[]{:S(2)}) async-start(f32[8,1,4]{2,1,0:T(1,128)} %bitcast.10), calls=%async_computation.3 | async-start | bytes 8192 | tf_op jit(solution)/shard_map/all_to_all | solution.py:79
  272.9 7.5 %copy-start.4 = (f32[1024,224]{0,1:T(8,128)S(1)}, f32[1024,224]{0,1:T(8,128)}, u32[]{:S(2)}) copy-start(f32[1024,224]{0,1:T(8,128)} %get-tuple-element.12) | copy-start | bytes 2752516
  280.4 6.9 %copy-start.2 = (bf16[1024,4096]{1,0:T(8,128)(2,1)S(1)}, bf16[1024,4096]{1,0:T(8,128)(2,1)}, u32[]{:S(2)}) copy-start(bf16[1024,4096]{1,0:T(8,128)(2,1)} %all-gather.3.cloned.1.call-done) | copy-start | bytes 25165828
Sparse Core Ops, SparseCore 0:
  24.9 79.0 all-gather.4
  107.1 77.8 all-gather.2
where the time goes:
time: 300 us
  blocking collectives  174 us (58%)
  waiting for transfers between devices  50.6 us (17%)
  matrix products  39.2 us (13%)
  between operations  15.4 us (5%)
  starting transfers between devices  9.87 us (3%)
  local copies, waits for them, and re-layouts  8.39 us (3%)
    unnamed x2, blocking collectives  153 us
    all_gather x1, waiting for transfers between devices, shards(): piece_dy = lax.all_gather(rows_dy, 'dp', axis=0, tiled=True)  48.4 us
    dot_general x3, matrix products, contract_rows(): lax.dot_general(left, right, (((0,), (0,)), ((), ())), preferred_element_...  17.9 us
    dot_general x3, matrix products, contract_cols(): lax.dot_general(left, right, (((1,), (1,)), ((), ())), preferred_element_...  17.5 us
    all_to_all x1, blocking collectives, shards(): lax.all_to_all(send_x.reshape(owners, ROW_CAPACITY, -1), 'expert', split_...  11.8 us
    all_to_all x1, blocking collectives, shards(): lax.all_to_all(send_dy.reshape(owners, ROW_CAPACITY, -1), 'expert', split...  9.57 us
  transfers between devices with their start and end apart: 4, of which 2 were waited for; matrix products, arithmetic and copies ran while one was open for 11% of the time, Pallas kernels for 0%

commit v1 on v0

--- a/solution.py
+++ b/solution.py
@@ -59,7 +59,8 @@
     up_local = up_w[0]
     down_local = down_w[0]
     piece_x = lax.all_gather(rows_x, "dp", axis=0, tiled=True)
-    piece_dy = lax.all_gather(rows_dy, "dp", axis=0, tiled=True)
+    stack = jnp.stack([rows_dy] * lax.axis_size("dp"))
+    piece_dy = jnp.concatenate(lax.all_to_all(stack, "dp", 0, 0), axis=0)
     piece_p = lax.all_gather(rows_p, "dp", axis=0, tiled=True)
     weight_p = piece_p.astype(jnp.float32)[:, None]
     gate_pre = contract_cols(piece_x, gate_local)

time: 300 us -> 469 us (1.56)
  blocking collectives: 174 us -> 363 us
  waiting for transfers between devices: 50.6 us -> 8.39 us
  starting transfers between devices: 9.87 us -> 25.5 us
    unnamed x2, blocking collectives: 153 us -> 351 us
    all_gather x1 -> x0, waiting for transfers between devices: 48.4 us -> none  [shards(): piece_dy = lax.all_gather(rows_dy, 'dp', axis=0, tiled=True)]
    all_to_all x0 -> x2, starting transfers between devices: none -> 15.5 us  [the longest x1 10.7 us: shards(): piece_dy = jnp.concatenate(lax.all_to_all(stack, 'dp', 0, 0), axis=0)]
    all_to_all x1 -> x0, blocking collectives: 9.57 us -> none  [shards(): lax.all_to_all(send_dy.reshape(owners, ROW_CAPACITY, -1), 'expert', split...]
  transfers between devices with their start and end apart: 4 -> 5, of which waited for: 2 -> 2; matrix products, arithmetic and copies ran while one was open for 11% -> 8% of each run, Pallas kernels for 0% -> 0%
where the time goes in v1:
time: 469 us; the launch traced here: 468 us
  blocking collectives  363 us (77%)
  matrix products  42.1 us (9%)
  starting transfers between devices  25.5 us (5%)
  between operations  15.5 us (3%)
  local copies, waits for them, and re-layouts  11.9 us (3%)
  waiting for transfers between devices  8.39 us (2%)
    unnamed x2, blocking collectives  351 us
    dot_general x3, matrix products, contract_rows(): lax.dot_general(left, right, (((0,), (0,)), ((), ())), preferred_element_...  20.8 us
    dot_general x3, matrix products, contract_cols(): lax.dot_general(left, right, (((1,), (1,)), ((), ())), preferred_element_...  17.4 us
    all_to_all x1, blocking collectives, shards(): lax.all_to_all(send_x.reshape(owners, ROW_CAPACITY, -1), 'expert', split_...  11.8 us
    all_to_all x1, starting transfers between devices, shards(): piece_dy = jnp.concatenate(lax.all_to_all(stack, 'dp', 0, 0), axis=0)  10.7 us
  transfers between devices with their start and end apart: 5, of which 2 were waited for; matrix products, arithmetic and copies ran while one was open for 8% of the time, Pallas kernels for 0%

profile of v1, /device:TPU:8, one launch (start us, length us, event | category | flops | bytes accessed | tf_op | source)
XLA Modules:
  0.0 468.0 jit_solution(15662143099130076043)
XLA Ops:
  7.2 0.0 copy-start
  7.2 0.0 all-gather.2.cloned.1.call-start
  7.2 0.9 copy.36
  8.1 0.1 eq.68
  8.3 0.1 eq.64
  8.4 0.6 reduce-window.6
  9.0 0.2 slice_reduce_fusion
  9.3 0.1 fusion.23
  9.4 0.1 reduce_sum.40
  9.5 0.2 gt.17
  9.7 0.1 copy.41
  9.8 0.1 copy.40
  9.8 0.7 add_select_fusion
  10.6 1.5 convolution_convert_fusion.2
  12.1 0.1 reshape.110
  12.2 11.8 %all_to_all.34 = bf16[8,4,4096]{2,1,0:T(4,128)(2,1)S(1)} all-to-all(bf16[8,4,4096]{2,1,0:T(4,128)(2,1)S(1)} %reshape.110), channel_id=1, replica_groups=mesh['dp'=32,'expert'=8] {'expert'}, dimensions={0} | all-to-all | bytes 524288 | tf_op jit(solution)/shard_map/all_to_all | solution.py:37
  24.0 0.8 reshape.111
  24.8 0.0 all-gather.2.cloned.1.call-update
  24.8 1.5 convolution_convert_fusion.3
  26.3 0.8 reshape.108
  27.1 4.8 %all-to-all-start.1 = ((bf16[8,4,4096]{2,1,0:T(4,128)(2,1)}), bf16[8,4,4096]{2,1,0:T(4,128)(2,1)S(1)}, u32[]{:S(2)}, u32[]{:S(2)}) async-start(bf16[8,4,4096]{2,1,0:T(4,128)(2,1)} %reshape.108), calls=%async_computation.1 | async-start | bytes 524288 | tf_op jit(solution)/shard_map/all_to_all | solution.py:44
  32.0 0.8 copy.38
  32.7 0.1 reshape.118
  32.9 0.1 fusion.12
  33.0 0.7 all_to_all.28
  33.7 3.8 all-to-all-done.1
  37.5 5.0 %all-to-all-start = ((bf16[8,1,4]{2,1,0:T(2,128)(2,1)}), bf16[8,1,4]{2,1,0:T(2,128)(2,1)S(1)}, u32[]{:S(2)}, u32[]{:S(2)}) async-start(bf16[8,1,4]{2,1,0:T(2,128)(2,1)} %all_to_all.28), calls=%async_computation | async-start | bytes 8192 | tf_op jit(solution)/shard_map/all_to_all | solution.py:51
  42.5 0.1 stack_reshape.2
  42.6 4.6 all-to-all-done
  47.2 4.3 stack.3
  51.4 0.0 copy-start.1
  51.4 10.7 %all-to-all-start.2 = ((bf16[32,32,4096]{2,1,0:T(8,128)(2,1)}), bf16[32,32,4096]{2,1,0:T(8,128)(2,1)}, u32[]{:S(2)}, u32[]{:S(2)}) async-start(bf16[32,32,4096]{2,1,0:T(8,128)(2,1)} %stack.3), calls=%async_computation.2 | async-start | bytes 16777216 | tf_op jit(solution)/shard_map/all_to_all | solution.py:63
  62.1 0.0 copy-done.1
  62.1 0.6 fusion.29
  64.0 0.1 reshape.113
  64.1 0.2 dynamic-update-slice
  64.4 280.9 %all-reduce = bf16[1024]{0:T(1024)(128)(2,1)S(1)} all-reduce(bf16[1024]{0:T(1024)(128)(2,1)S(1)} %dynamic-update-slice), channel_id=1, replica_groups=mesh['dp'=32,'expert'=8] {'dp'}, use_global_device_ids=true, to_apply=%add | all-reduce | flops 1024 | bytes 4096
  345.3 0.0 all-gather.2.cloned.1.call-done
  345.3 0.0 copy-start.2
  345.3 0.0 copy-start.3
  345.3 6.7 %fusion.6 = f32[1024,224]{0,1:T(8,128)S(1)} fusion(bf16[1024,4096]{1,0:T(8,128)(2,1)} %all-gather.2.cloned.1.call-done, bf16[1,224,4096]{2,1,0:T(8,128)(2,1)} %param.11), kind=kOutput, calls=%fused_computation.11 | convolution fusion | flops 1879048192 | bytes 11141120 | tf_op jit(solution)/shard_map/dot_general | solution.py:16
  352.0 0.0 copy-done.2
  352.0 0.1 copy-done.3
  352.1 3.6 fusion.8
  355.7 0.0 all-to-all-done.2
  355.7 0.0 copy-done
  355.7 7.2 %multiply_reduce_fusion = (f32[1024]{0:T(1024)S(1)}, bf16[1024,224]{0,1:T(8,128)(2,1)S(1)}, f32[1024,224]{0,1:T(8,128)}) fusion(f32[1024,224]{0,1:T(8,128)} %fusion.8, f32[1024,224]{0,1:T(8,128)S(1)} %fusion.6, bf16[1024,4096]{1,0:T(8,128)(2,1)} %bitcast.4, bf16[1,224,4096]{2,1,0:T(8,128)(2,1)S(1)} %copy-done), kind=kOutput, calls=%fused_computation.19 | convolution fusion | flops 1881111552 | bytes 13438976 | tf_op jit(solution)/shard_map/dot_general | solution.py:16
  362.8 69.9 %all-reduce.1 = f32[1024]{0:T(1024)S(1)} all-reduce(f32[1024]{0:T(1024)S(1)} %get-tuple-element.6), channel_id=2, replica_groups=mesh['dp'=32,'expert'=8] {'dp'}, use_global_device_ids=true, to_apply=%region_6.7.clone | all-reduce | flops 1024 | bytes 8192
  432.7 0.1 dynamic-slice.2
  432.8 0.7 all_to_all.26
  433.4 4.9 %all-to-all-start.4 = ((f32[8,1,4]{2,1,0:T(1,128)}), f32[8,1,4]{2,1,0:T(1,128)S(1)}, u32[]{:S(2)}, u32[]{:S(2)}) async-start(f32[8,1,4]{2,1,0:T(1,128)} %bitcast.11), calls=%async_computation.4 | async-start | bytes 8192 | tf_op jit(solution)/shard_map/all_to_all | solution.py:80
  438.4 0.0 copy-start.4
  438.4 0.0 copy-start.5
  438.4 7.2 %fusion.4 = bf16[1,224,4096]{2,1,0:T(8,128)(2,1)} fusion(bf16[1024,4096]{1,0:T(8,128)(2,1)} %all-gather.2.cloned.1.call-done, f32[1024,224]{0,1:T(8,128)S(1)} %fusion.6, f32[1024,224]{0,1:T(8,128)} %get-tuple-element.12, f32[1024]{0:T(1024)S(1)} %convert_element_type.63), kind=kOutput, calls=%fused_computation.7 | convolution fusion | flops 1881571328 | bytes 12062720 | tf_op jit(solution)/shard_map/dot_general | solution.py:10
  445.5 0.0 copy-done.4
  445.5 0.0 copy-done.5
  445.5 6.9 %fusion.3 = bf16[1,224,4096]{2,1,0:T(8,128)(2,1)} fusion(bf16[1024,4096]{1,0:T(8,128)(2,1)} %all-gather.2.cloned.1.call-done, f32[1024,224]{0,1:T(8,128)S(1)} %fusion.6, f32[1024,224]{0,1:T(8,128)S(1)} %copy-done.4, f32[1024,224]{0,1:T(8,128)S(1)} %copy-done.5, f32[1024]{0:T(1024)S(1)} %convert_element_type.63), kind=kOutput, calls=%fused_computation.6 | convolution fusion | flops 1882488832 | bytes 12980224 | tf_op jit(solution)/shard_map/dot_general | solution.py:10
  452.4 6.8 %fusion.5 = bf16[1,224,4096]{2,1,0:T(8,128)(2,1)} fusion(bf16[1024,224]{0,1:T(8,128)(2,1)S(1)} %get-tuple-element.7, bf16[1024,4096]{1,0:T(8,128)(2,1)} %bitcast.4, f32[1024]{0:T(1024)S(1)} %convert_element_type.63), kind=kOutput, calls=%fused_computation.8 | convolution fusion | flops 1892548608 | bytes 10686464 | tf_op jit(solution)/shard_map/dot_general | solution.py:10
  459.2 0.0 all-to-all-done.4
  459.2 0.5 broadcast.76
  459.7 0.7 reduce.6
  460.4 0.1 reshape.120
  460.5 0.7 fusion.18
  (8 shorter events, 0.1 us)
Async XLA Ops:
  7.2 348.5 %copy-start = (bf16[1,224,4096]{2,1,0:T(8,128)(2,1)S(1)}, bf16[1,224,4096]{2,1,0:T(8,128)(2,1)}, u32[]{:S(2)}) copy-start(bf16[1,224,4096]{2,1,0:T(8,128)(2,1)} %param.13) | copy-start | bytes 5505028
  7.2 338.1 %all-gather.2.cloned.1.call-start = ((), (), s32[]{:S(2)}) async-start(), calls=%async_computation.5 | async-start | bytes 8650752 | tf_op jit(solution)/shard_map/all_gather | solution.py:61
  27.1 10.4 %all-to-all-start.1 = ((bf16[8,4,4096]{2,1,0:T(4,128)(2,1)}), bf16[8,4,4096]{2,1,0:T(4,128)(2,1)S(1)}, u32[]{:S(2)}, u32[]{:S(2)}) async-start(bf16[8,4,4096]{2,1,0:T(4,128)(2,1)} %reshape.108), calls=%async_computation.1 | async-start | bytes 524288 | tf_op jit(solution)/shard_map/all_to_all | solution.py:44
  37.5 9.7 %all-to-all-start = ((bf16[8,1,4]{2,1,0:T(2,128)(2,1)}), bf16[8,1,4]{2,1,0:T(2,128)(2,1)S(1)}, u32[]{:S(2)}, u32[]{:S(2)}) async-start(bf16[8,1,4]{2,1,0:T(2,128)(2,1)} %all_to_all.28), calls=%async_computation | async-start | bytes 8192 | tf_op jit(solution)/shard_map/all_to_all | solution.py:51
  51.4 10.7 %copy-start.1 = (u32[256]{0:T(256)S(1)}, u32[256]{0:T(256)}, u32[]{:S(2)}) copy-start(u32[256]{0:T(256)} %constant.24) | copy-start | bytes 3076
  51.4 304.2 %all-to-all-start.2 = ((bf16[32,32,4096]{2,1,0:T(8,128)(2,1)}), bf16[32,32,4096]{2,1,0:T(8,128)(2,1)}, u32[]{:S(2)}, u32[]{:S(2)}) async-start(bf16[32,32,4096]{2,1,0:T(8,128)(2,1)} %stack.3), calls=%async_computation.2 | async-start | bytes 16777216 | tf_op jit(solution)/shard_map/all_to_all | solution.py:63
  345.3 6.7 %copy-start.2 = (bf16[1024,4096]{1,0:T(8,128)(2,1)S(1)}, bf16[1024,4096]{1,0:T(8,128)(2,1)}, u32[]{:S(2)}) copy-start(bf16[1024,4096]{1,0:T(8,128)(2,1)} %all-gather.2.cloned.1.call-done) | copy-start | bytes 25165828
  345.3 6.8 %copy-start.3 = (bf16[1,224,4096]{2,1,0:T(8,128)(2,1)S(1)}, bf16[1,224,4096]{2,1,0:T(8,128)(2,1)}, u32[]{:S(2)}) copy-start(bf16[1,224,4096]{2,1,0:T(8,128)(2,1)} %param.12) | copy-start | bytes 5505028
  433.4 25.8 %all-to-all-start.4 = ((f32[8,1,4]{2,1,0:T(1,128)}), f32[8,1,4]{2,1,0:T(1,128)S(1)}, u32[]{:S(2)}, u32[]{:S(2)}) async-start(f32[8,1,4]{2,1,0:T(1,128)} %bitcast.11), calls=%async_computation.4 | async-start | bytes 8192 | tf_op jit(solution)/shard_map/all_to_all | solution.py:80
  438.4 7.2 %copy-start.4 = (f32[1024,224]{0,1:T(8,128)S(1)}, f32[1024,224]{0,1:T(8,128)}, u32[]{:S(2)}) copy-start(f32[1024,224]{0,1:T(8,128)} %fusion.8) | copy-start | bytes 2752516
  438.4 7.2 %copy-start.5 = (f32[1024,224]{0,1:T(8,128)S(1)}, f32[1024,224]{0,1:T(8,128)}, u32[]{:S(2)}) copy-start(f32[1024,224]{0,1:T(8,128)} %get-tuple-element.12) | copy-start | bytes 2752516
Sparse Core Ops, SparseCore 0:
  24.9 228.7 all-gather.1
